TPU v7x, 512 devices: a whole 4x4x16 slice. The times are simulated.
512 devices in a mesh: gx: 32 (over z, core), gy: 4 (over x), gz: 4 (over y).
Axes of the slice: x: 4, y: 4, z: 16, core: 2. Of those that a mesh axis runs over, the one named last changes fastest.
Arguments:
- source_field: float32 [3, 256, 32, 512], P(None, 'gx', 'gy', 'gz'), may hold values from -6 to 6
- cell_contrast: bfloat16 [65536, 1536], P(('gx', 'gy', 'gz')), may hold values from 0.19921875 to 2
- point_field: bfloat16 [3, 65536], P(None, ('gx', 'gy', 'gz')), may hold values from -3 to 3
- point_class: int32 [65536, 1], P(('gx', 'gy', 'gz')), may hold values from 0 to 31; in each aligned block of 128 rows (0 to 127, 128 to 255, ...) at most 8 rows name the same one
- cell_kind: int32 [65536], P(('gx', 'gy', 'gz')), may hold values from 0 to 3
- inverse_blocks: float32 [32, 4, 3, 3, 512], P('gx'), may hold values from -0.3 to 0.3
Outputs:
- newton_step: float32 [3, 256, 32, 512], P(None, 'gx', 'gy', 'gz')
- krylov_residual: float32 [3, 256, 32, 512], P(None, 'gx', 'gy', 'gz')
Inputs may be any that keep to these rules, and one draw needn't show every extreme that they name: `point_class`: among the 128 points of one device's block no class is named more than 8 times, a bound that some block reaches there.
All inputs are finite; a program needn't handle non-finite values.
Results may differ from a plain program's by a relative error of at most 0.0076.
Values may be sent and summed in bfloat16 or wider, within the bound.
A program may use at most 64 MiB of HBM per device.

v0:
```python
import math
import jax
import jax.numpy as jnp
from jax import lax
from jax.sharding import PartitionSpec as P

CELL = 8
VOX = 512
TYPES = 4
ZP = 8
ITERS = 3
kerr_scale = 0.1


def with_halo(block, sides, width):
    for axis, dim in sides:
        count = lax.axis_size(axis)
        forward = [(i, i + 1) for i in range(count - 1)]
        backward = [(target, source) for source, target in forward]
        low = lax.ppermute(
            lax.slice_in_dim(block, block.shape[dim] - width, None, axis=dim), axis, forward
        )
        high = lax.ppermute(lax.slice_in_dim(block, 0, width, axis=dim), axis, backward)
        block = jnp.concatenate([low, block, high], axis=dim)
    return block


def hartley_table():
    voxel_index = jnp.arange(VOX, dtype=jnp.int32)
    along_one = voxel_index // (CELL * CELL)
    along_two = voxel_index // CELL % CELL
    along_three = voxel_index % CELL
    phase_index = (
        along_one[:, None] * along_one[None, :]
        + along_two[:, None] * along_two[None, :]
        + along_three[:, None] * along_three[None, :]
    ) % CELL
    phase_angle = 2.0 * math.pi / CELL * phase_index.astype(jnp.float32)
    return ((jnp.cos(phase_angle) + jnp.sin(phase_angle)) / math.sqrt(VOX)).astype(jnp.bfloat16)


def cell_solve(contrast, point_values, blocks, hartley):
    row_count = contrast.shape[0]
    weights = contrast.reshape(row_count, 3, VOX).astype(jnp.float32)
    base_field = point_values.astype(jnp.float32)[:, :, None]

    def correction(polarization):
        spectrum = jnp.dot(
            polarization.reshape(row_count * 3, VOX), hartley, preferred_element_type=jnp.float32
        ).reshape(row_count, 3, VOX)
        mixed_spectrum = jnp.sum(blocks * spectrum[:, None, :, :], axis=2).astype(jnp.bfloat16)
        return jnp.dot(
            mixed_spectrum.reshape(row_count * 3, VOX), hartley, preferred_element_type=jnp.float32
        ).reshape(row_count, 3, VOX)

    local_field = base_field - correction((weights * base_field).astype(jnp.bfloat16))
    kerr_polar = (weights * local_field * (1.0 + kerr_scale * local_field * local_field)).astype(
        jnp.bfloat16
    )
    final_field = base_field - correction(kerr_polar)
    flux_mean = jnp.mean((1.0 + weights) * final_field, axis=2)
    stiffness = 0.5 + jnp.mean(weights * final_field * final_field, axis=(1, 2))
    return jnp.concatenate([flux_mean, stiffness[:, None]], axis=1)


def solve_batched(contrast, point_values, keys, library, hartley):
    return cell_solve(contrast, point_values, library[keys], hartley)


def operate(field, diagonal):
    padded = with_halo(field, (("gx", 1), ("gy", 2), ("gz", 3)), 1)
    beside = padded[:, 2:, 1:-1, 1:-1] + padded[:, :-2, 1:-1, 1:-1]
    beside = beside + padded[:, 1:-1, 2:, 1:-1] + padded[:, 1:-1, :-2, 1:-1]
    beside = beside + padded[:, 1:-1, 1:-1, 2:] + padded[:, 1:-1, 1:-1, :-2]
    return (6.0 + diagonal)[None] * field - beside


def squares(residual):
    return lax.psum(jnp.sum(residual * residual), ("gx", "gy", "gz"))


def per_device(source_field, cell_contrast, point_field, point_class, cell_kind, inverse_blocks):
    hartley = hartley_table()
    point_values = point_field.T
    library = lax.all_gather(inverse_blocks, "gx", axis=0, tiled=True)
    library = library.reshape(library.shape[0] * library.shape[1], 3, 3, VOX)
    chosen = point_class[:, 0] * TYPES + cell_kind
    summary = solve_batched(cell_contrast, point_values, chosen, library, hartley)
    extent_x = source_field.shape[1]
    extent_y = source_field.shape[2]
    extent_z = source_field.shape[3]
    blocks_z = extent_z // ZP
    stiffness_grid = jnp.broadcast_to(
        summary[:, 3].reshape(1, extent_y, blocks_z, 1), (extent_x, extent_y, blocks_z, ZP)
    ).reshape(extent_x, extent_y, extent_z)
    flux_grid = jnp.broadcast_to(
        summary[:, :3].T.reshape(3, 1, extent_y, blocks_z, 1), (3, extent_x, extent_y, blocks_z, ZP)
    ).reshape(3, extent_x, extent_y, extent_z)
    right = source_field - flux_grid
    newton_step = jnp.zeros_like(right)
    residual = right
    direction = right
    norm_now = squares(residual)
    for iteration in range(ITERS):
        image = operate(direction, stiffness_grid)
        alpha = norm_now / lax.psum(jnp.sum(direction * image), ("gx", "gy", "gz"))
        newton_step = newton_step + alpha * direction
        residual = residual - alpha * image
        norm_next = squares(residual)
        direction = residual + norm_next / norm_now * direction
        norm_now = norm_next
    return (newton_step, residual)


def solution(mesh):
    placed = (
        P(None, "gx", "gy", "gz"),
        P(("gx", "gy", "gz"), None),
        P(None, ("gx", "gy", "gz")),
        P(("gx", "gy", "gz"), None),
        P(("gx", "gy", "gz")),
        P("gx", None, None, None, None),
    )
    return jax.shard_map(
        per_device,
        mesh=mesh,
        in_specs=placed,
        out_specs=(P(None, "gx", "gy", "gz"), P(None, "gx", "gy", "gz")),
        check_vma=False,
    )
```

profile of v0, /device:TPU:1, one launch (start us, length us, event | category | flops | bytes accessed | tf_op | source)
XLA Modules:
  0.0 722.5 jit_solution(11703445166906747007)
XLA Ops:
  10.1 4.7 fusion.12
  16.4 71.8 %all-gather.2.cloned.1.call-done = f32[32,4,3,3,512]{4,1,3,2,0:T(4,128)} async-done(((f32[1,4,3,3,512]{4,1,3,2,0:T(4,128)}), f32[32,4,3,3,512]{4,1,3,2,0:T(4,128)}) %all-gather.2.cloned.1.call-update) | async-done | bytes 2359312 | tf_op jit(solution)/shard_map/all_gather | solution.py:85
  88.2 4.6 copy.45
  92.7 4.3 gather_fusion
  97.1 4.6 multiply_reduce_fusion.1
  101.7 11.6 %fusion.7 = f32[128,3,512]{2,0,1:T(8,128)} fusion(f32[128,3,512]{2,0,1:T(8,128)} %copy-done.1, s32[512]{0:T(512)S(1)} %get-tuple-element.33, s32[512]{0:T(512)S(1)} %get-tuple-element.34, s32[512]{0:T(512)S(1)} %add_select_fusion.4, bf16[128,3,512]{2,1,0:T(4,128)(2,1)} %multiply_reduce_fusion.1, f32[128,3]{0,1:T(4,128)S(1)} %convert_bitcast_fusion), kind=kOutput, calls=%fused_computation.21 | convolution fusion | flops 415039488 | bytes 1973760 | tf_op jit(solution)/shard_map/dot_general | solution.py:48
  113.3 1.7 copy.42
  115.0 3.7 multiply_reduce_fusion
  118.7 4.9 fusion.6
  124.0 2.2 collective-permute-start
  126.2 3.4 collective-permute-start.1
  131.8 4.0 collective-permute-start.3
  136.8 3.1 collective-permute-start.5
  141.5 3.6 collective-permute-done.5
  145.1 3.8 collective-permute-done.4
  149.7 102.9 %all-reduce = (f32[]{:T(128)}, f32[]{:T(128)}) all-reduce(f32[]{:T(128)} %get-tuple-element.5, f32[]{:T(128)} %get-tuple-element.4), channel_id=1, replica_groups=mesh['gx'=32,'gy'=4,'gz'=4] {'gx','gy','gz'}, use_global_device_ids=true, to_apply=%region_4.5 | all-reduce | flops 2 | bytes 16 | tf_op jit(solution)/shard_map/psum | solution.py:79
  254.6 100.5 %psum.44 = f32[]{:T(128)} all-reduce(f32[]{:T(128)} %multiply_reduce_fusion.6), channel_id=1, replica_groups=mesh['gx'=32,'gy'=4,'gz'=4] {'gx','gy','gz'}, use_global_device_ids=true, to_apply=%region_9.10 | all-reduce | flops 1 | bytes 8 | tf_op jit(solution)/shard_map/psum | solution.py:79
  356.5 2.6 collective-permute-start.6
  359.1 3.0 collective-permute-start.7
  364.2 4.0 collective-permute-start.9
  369.2 2.5 collective-permute-start.11
  373.1 3.5 collective-permute-done.11
  376.5 3.8 collective-permute-done.10
  381.2 101.6 %psum.45 = f32[]{:T(128)} all-reduce(f32[]{:T(128)} %get-tuple-element.12), channel_id=1, replica_groups=mesh['gx'=32,'gy'=4,'gz'=4] {'gx','gy','gz'}, use_global_device_ids=true, to_apply=%region_11.12 | all-reduce | flops 1 | bytes 8 | tf_op jit(solution)/shard_map/psum | solution.py:106
  484.8 100.4 %psum.46 = f32[]{:T(128)} all-reduce(f32[]{:T(128)} %get-tuple-element.10), channel_id=1, replica_groups=mesh['gx'=32,'gy'=4,'gz'=4] {'gx','gy','gz'}, use_global_device_ids=true, to_apply=%region_13.14 | all-reduce | flops 1 | bytes 8 | tf_op jit(solution)/shard_map/psum | solution.py:79
  586.5 2.6 collective-permute-start.12
  589.1 3.0 collective-permute-start.13
  594.2 4.0 collective-permute-start.15
  599.2 2.4 collective-permute-start.17
  602.9 3.5 collective-permute-done.17
  606.4 3.8 collective-permute-done.16
  611.0 101.6 %psum.47 = f32[]{:T(128)} all-reduce(f32[]{:T(128)} %get-tuple-element.8), channel_id=1, replica_groups=mesh['gx'=32,'gy'=4,'gz'=4] {'gx','gy','gz'}, use_global_device_ids=true, to_apply=%region_15.16 | all-reduce | flops 1 | bytes 8 | tf_op jit(solution)/shard_map/psum | solution.py:106
  (68 shorter events, 23.3 us)
Async XLA Ops:
  7.2 81.0 %all-gather.2.cloned.1.call-start = ((), (), s32[]{:S(2)}) async-start(), calls=%async_computation | async-start | bytes 2433024 | tf_op jit(solution)/shard_map/all_gather | solution.py:85
  9.3 5.5 copy-start.1
  10.1 6.3 copy-start.3
  10.1 6.3 copy-start.4
  113.3 5.4 copy-start.2
  118.7 5.3 copy-start
  124.0 5.6 collective-permute-start
  126.2 4.2 collective-permute-start.1
  130.5 5.3 collective-permute-start.2
  131.8 4.8 collective-permute-start.3
  136.8 8.3 %collective-permute-start.5 = (f32[3,10,10,1]{3,2,1,0:T(8,128)S(1)}, f32[3,10,10,1]{3,2,1,0:T(8,128)S(1)}, u32[]{:S(2)}, u32[]{:S(2)}) collective-permute-start(f32[3,10,10,1]{3,2,1,0:T(8,128)S(1)} %get-tuple-element.20), channel_id=1, source_target_pairs={{0,1},{1,2},{2,3},{4,5},{5,6},{6,7},{8,9},{9,10},{10,11},{12,13},{... | collective-permute-start | bytes 3608 | tf_op jit(solution)/shard_map/ppermute | solution.py:20
  139.9 9.0 %collective-permute-start.4 = (f32[3,10,10,1]{3,2,1,0:T(8,128)S(1)}, f32[3,10,10,1]{3,2,1,0:T(8,128)S(1)}, u32[]{:S(2)}, u32[]{:S(2)}) collective-permute-start(f32[3,10,10,1]{3,2,1,0:T(8,128)S(1)} %get-tuple-element.19), channel_id=1, source_target_pairs={{1,0},{2,1},{3,2},{5,4},{6,5},{7,6},{9,8},{10,9},{11,10},{13,12},{... | collective-permute-start | bytes 3608 | tf_op jit(solution)/shard_map/ppermute | solution.py:23
  356.5 5.6 collective-permute-start.6
  359.1 3.8 collective-permute-start.7
  362.9 5.3 collective-permute-start.8
  364.2 4.8 collective-permute-start.9
  369.2 7.3 %collective-permute-start.11 = (f32[3,10,10,1]{3,2,1,0:T(8,128)S(1)}, f32[3,10,10,1]{3,2,1,0:T(8,128)S(1)}, u32[]{:S(2)}, u32[]{:S(2)}) collective-permute-start(f32[3,10,10,1]{3,2,1,0:T(8,128)S(1)} %get-tuple-element.18), channel_id=1, source_target_pairs={{0,1},{1,2},{2,3},{4,5},{5,6},{6,7},{8,9},{9,10},{10,11},{12,13},{... | collective-permute-start | bytes 3608 | tf_op jit(solution)/shard_map/ppermute | solution.py:20
  371.8 8.6 %collective-permute-start.10 = (f32[3,10,10,1]{3,2,1,0:T(8,128)S(1)}, f32[3,10,10,1]{3,2,1,0:T(8,128)S(1)}, u32[]{:S(2)}, u32[]{:S(2)}) collective-permute-start(f32[3,10,10,1]{3,2,1,0:T(8,128)S(1)} %get-tuple-element.17), channel_id=1, source_target_pairs={{1,0},{2,1},{3,2},{5,4},{6,5},{7,6},{9,8},{10,9},{11,10},{13,12},{... | collective-permute-start | bytes 3608 | tf_op jit(solution)/shard_map/ppermute | solution.py:23
  586.5 5.6 collective-permute-start.12
  589.1 3.8 collective-permute-start.13
  592.9 5.3 collective-permute-start.14
  594.2 4.8 collective-permute-start.15
  599.2 7.2 collective-permute-start.17
  601.6 8.6 %collective-permute-start.16 = (f32[3,10,10,1]{3,2,1,0:T(8,128)S(1)}, f32[3,10,10,1]{3,2,1,0:T(8,128)S(1)}, u32[]{:S(2)}, u32[]{:S(2)}) collective-permute-start(f32[3,10,10,1]{3,2,1,0:T(8,128)S(1)} %get-tuple-element.15), channel_id=1, source_target_pairs={{1,0},{2,1},{3,2},{5,4},{6,5},{7,6},{9,8},{10,9},{11,10},{13,12},{... | collective-permute-start | bytes 3608 | tf_op jit(solution)/shard_map/ppermute | solution.py:23
Sparse Core Ops, SparseCore 0:
  10.1 78.0 all-gather.1
where the time goes:
time: 733 us; the launch traced here: 723 us
  blocking collectives  507 us (69%)
  waiting for transfers between devices  99.3 us (14%)
  starting transfers between devices  44.5 us (6%)
  between operations  21.5 us (3%)
  matrix products  21.3 us (3%)
  local copies, waits for them, and re-layouts  14.6 us (2%)
  other arithmetic  14.3 us (2%)
    psum x3, blocking collectives, squares(): return lax.psum(jnp.sum(residual * residual), ('gx', 'gy', 'gz'))  304 us
    psum x2, blocking collectives, per_device(): alpha = norm_now / lax.psum(jnp.sum(direction * image), ('gx', 'gy', 'gz'))  203 us
    all_gather x1, waiting for transfers between devices, per_device(): library = lax.all_gather(inverse_blocks, 'gx', axis=0, tiled=True)  71.8 us
    ppermute x9, starting transfers between devices, with_halo(): lax.ppermute(lax.slice_in_dim(block, block.shape[dim] - width, None, axis...  29.4 us
    dot_general x2, matrix products, correction(): jnp.dot(polarization.reshape(row_count * 3, VOX), hartley, preferred_elem...  16.3 us
    ppermute x9, waiting for transfers between devices, with_halo(): lax.ppermute(lax.slice_in_dim(block, block.shape[dim] - width, None, axis...  15.4 us
    ppermute x9, starting transfers between devices, with_halo(): lax.ppermute(lax.slice_in_dim(block, 0, width, axis=dim), axis, backward)  15.1 us
  transfers between devices with their start and end apart: 19, of which 13 were waited for; matrix products, arithmetic and copies ran while one was open for 1% of the time, Pallas kernels for 0%

commit v1 on v0

--- a/solution.py
+++ b/solution.py
@@ -82,7 +82,9 @@
 def per_device(source_field, cell_contrast, point_field, point_class, cell_kind, inverse_blocks):
     hartley = hartley_table()
     point_values = point_field.T
-    library = lax.all_gather(inverse_blocks, "gx", axis=0, tiled=True)
+    all_rows = lax.psum(1, axis_name="gx")
+    step_out = jnp.concatenate([inverse_blocks] * all_rows, axis=0)
+    library = lax.all_to_all(step_out, axis_name="gx", split_axis=0, concat_axis=0, tiled=True)
     library = library.reshape(library.shape[0] * library.shape[1], 3, 3, VOX)
     chosen = point_class[:, 0] * TYPES + cell_kind
     summary = solve_batched(cell_contrast, point_values, chosen, library, hartley)

time: 733 us -> 765 us (1.044)
  waiting for transfers between devices: 99.3 us -> 127 us
  starting transfers between devices: 44.5 us -> 64.1 us
  between operations: 21.5 us -> 8.14 us
    all_to_all x0 -> x1, waiting for transfers between devices: none -> 100 us  [per_device(): lax.all_to_all(step_out, axis_name='gx', split_axis=0, concat_axis=0, til...]
    all_gather x1 -> x0, waiting for transfers between devices: 71.8 us -> none  [per_device(): library = lax.all_gather(inverse_blocks, 'gx', axis=0, tiled=True)]
    all_to_all x0 -> x1, starting transfers between devices: none -> 16.9 us  [per_device(): lax.all_to_all(step_out, axis_name='gx', split_axis=0, concat_axis=0, til...]
where the time goes in v1:
time: 765 us; the launch traced here: 754 us
  blocking collectives  504 us (66%)
  waiting for transfers between devices  127 us (17%)
  starting transfers between devices  64.1 us (8%)
  matrix products  22.4 us (3%)
  local copies, waits for them, and re-layouts  15.4 us (2%)
  other arithmetic  13.6 us (2%)
  between operations  8.14 us (1%)
    psum x3, blocking collectives, squares(): return lax.psum(jnp.sum(residual * residual), ('gx', 'gy', 'gz'))  301 us
    psum x2, blocking collectives, per_device(): alpha = norm_now / lax.psum(jnp.sum(direction * image), ('gx', 'gy', 'gz'))  203 us
    all_to_all x1, waiting for transfers between devices, per_device(): lax.all_to_all(step_out, axis_name='gx', split_axis=0, concat_axis=0, til...  100 us
    ppermute x9, starting transfers between devices, with_halo(): lax.ppermute(lax.slice_in_dim(block, block.shape[dim] - width, None, axis...  31.6 us
    dot_general x2, matrix products, correction(): jnp.dot(polarization.reshape(row_count * 3, VOX), hartley, preferred_elem...  17.5 us
    all_to_all x1, starting transfers between devices, per_device(): lax.all_to_all(step_out, axis_name='gx', split_axis=0, concat_axis=0, til...  16.9 us
    ppermute x9, starting transfers between devices, with_halo(): lax.ppermute(lax.slice_in_dim(block, 0, width, axis=dim), axis, backward)  15.6 us
  transfers between devices with their start and end apart: 19, of which 13 were waited for; matrix products, arithmetic and copies ran while one was open for 1% of the time, Pallas kernels for 0%

profile of v1, /device:TPU:1, one launch (start us, length us, event | category | flops | bytes accessed | tf_op | source)
XLA Modules:
  0.0 754.4 jit_solution(16817240499726245476)
XLA Ops:
  0.6 2.7 concatenate.78
  3.3 16.9 %all-to-all-start = ((f32[32,4,3,3,512]{4,1,3,2,0:T(4,128)}), f32[32,4,3,3,512]{4,1,3,2,0:T(4,128)S(1)}, u32[]{:S(2)}, u32[]{:S(2)}) async-start(f32[32,4,3,3,512]{4,1,3,2,0:T(4,128)} %concatenate.78), calls=%async_computation | async-start | bytes 4718592 | tf_op jit(solution)/shard_map/all_to_all | solution.py:87
  21.5 5.9 fusion.12
  29.0 100.4 %all-to-all-done = f32[32,4,3,3,512]{4,1,3,2,0:T(4,128)S(1)} async-done(((f32[32,4,3,3,512]{4,1,3,2,0:T(4,128)}), f32[32,4,3,3,512]{4,1,3,2,0:T(4,128)S(1)}, u32[]{:S(2)}, u32[]{:S(2)}) %all-to-all-start) | async-done | bytes 2359328 | tf_op jit(solution)/shard_map/all_to_all | solution.py:87
  129.4 2.9 copy.59
  132.3 4.3 gather_fusion
  136.6 4.6 multiply_reduce_fusion.1
  141.2 11.6 %fusion.7 = f32[128,3,512]{2,0,1:T(8,128)} fusion(f32[128,3,512]{2,0,1:T(8,128)} %copy.49, s32[512]{0:T(512)S(1)} %get-tuple-element.33, s32[512]{0:T(512)S(1)} %get-tuple-element.34, s32[512]{0:T(512)S(1)} %add_select_fusion.4, bf16[128,3,512]{2,1,0:T(4,128)(2,1)} %multiply_reduce_fusion.1, f32[128,3]{0,1:T(4,128)S(1)} %convert_bitcast_fusion), kind=kOutput, calls=%fused_computation.21 | convolution fusion | flops 415039488 | bytes 1973760 | tf_op jit(solution)/shard_map/dot_general | solution.py:48
  154.6 3.7 multiply_reduce_fusion
  158.2 4.9 fusion.6
  163.6 2.7 collective-permute-start
  166.3 5.0 collective-permute-start.1
  173.5 4.0 collective-permute-start.3
  178.5 3.2 collective-permute-start.5
  183.3 3.1 collective-permute-done.5
  186.5 4.1 collective-permute-done.4
  191.4 102.5 %all-reduce = (f32[]{:T(128)}, f32[]{:T(128)}) all-reduce(f32[]{:T(128)} %get-tuple-element.5, f32[]{:T(128)} %get-tuple-element.4), channel_id=1, replica_groups=mesh['gx'=32,'gy'=4,'gz'=4] {'gx','gy','gz'}, use_global_device_ids=true, to_apply=%region_4.5 | all-reduce | flops 2 | bytes 16 | tf_op jit(solution)/shard_map/psum | solution.py:79
  295.8 98.7 %psum.44 = f32[]{:T(128)} all-reduce(f32[]{:T(128)} %multiply_reduce_fusion.6), channel_id=1, replica_groups=mesh['gx'=32,'gy'=4,'gz'=4] {'gx','gy','gz'}, use_global_device_ids=true, to_apply=%region_9.10 | all-reduce | flops 1 | bytes 8 | tf_op jit(solution)/shard_map/psum | solution.py:79
  395.9 2.6 collective-permute-start.6
  398.5 3.5 collective-permute-start.7
  404.1 4.0 collective-permute-start.9
  409.2 2.5 collective-permute-start.11
  413.0 3.5 collective-permute-done.11
  416.5 3.8 collective-permute-done.10
  421.1 101.1 %psum.45 = f32[]{:T(128)} all-reduce(f32[]{:T(128)} %get-tuple-element.12), channel_id=1, replica_groups=mesh['gx'=32,'gy'=4,'gz'=4] {'gx','gy','gz'}, use_global_device_ids=true, to_apply=%region_11.12 | all-reduce | flops 1 | bytes 8 | tf_op jit(solution)/shard_map/psum | solution.py:108
  524.2 99.6 %psum.46 = f32[]{:T(128)} all-reduce(f32[]{:T(128)} %get-tuple-element.10), channel_id=1, replica_groups=mesh['gx'=32,'gy'=4,'gz'=4] {'gx','gy','gz'}, use_global_device_ids=true, to_apply=%region_13.14 | all-reduce | flops 1 | bytes 8 | tf_op jit(solution)/shard_map/psum | solution.py:79
  625.2 2.6 collective-permute-start.12
  627.8 3.0 collective-permute-start.13
  632.9 4.0 collective-permute-start.15
  641.6 3.5 collective-permute-done.17
  645.1 3.8 collective-permute-done.16
  649.7 101.7 %psum.47 = f32[]{:T(128)} all-reduce(f32[]{:T(128)} %get-tuple-element.8), channel_id=1, replica_groups=mesh['gx'=32,'gy'=4,'gz'=4] {'gx','gy','gz'}, use_global_device_ids=true, to_apply=%region_15.16 | all-reduce | flops 1 | bytes 8 | tf_op jit(solution)/shard_map/psum | solution.py:108
  (70 shorter events, 25.9 us)
Async XLA Ops:
  0.6 19.6 %copy-start.2 = (bf16[128,1536]{1,0:T(8,128)(2,1)S(1)}, bf16[128,1536]{1,0:T(8,128)(2,1)}, u32[]{:S(2)}) copy-start(bf16[128,1536]{1,0:T(8,128)(2,1)} %param.7) | copy-start | bytes 1179652
  3.3 18.2 %copy-start.3 = (bf16[3,128]{1,0:T(4,128)(2,1)S(1)}, bf16[3,128]{1,0:T(4,128)(2,1)}, u32[]{:S(2)}) copy-start(bf16[3,128]{1,0:T(4,128)(2,1)} %param.8) | copy-start | bytes 2308
  3.3 126.1 %all-to-all-start = ((f32[32,4,3,3,512]{4,1,3,2,0:T(4,128)}), f32[32,4,3,3,512]{4,1,3,2,0:T(4,128)S(1)}, u32[]{:S(2)}, u32[]{:S(2)}) async-start(f32[32,4,3,3,512]{4,1,3,2,0:T(4,128)} %concatenate.78), calls=%async_computation | async-start | bytes 4718592 | tf_op jit(solution)/shard_map/all_to_all | solution.py:87
  21.5 7.4 copy-start.4
  21.5 7.4 copy-start.5
  152.8 5.4 copy-start.1
  158.2 5.3 copy-start
  163.6 7.8 %collective-permute-start = (f32[3,1,8,128]{3,2,1,0:T(8,128)S(1)}, f32[3,1,8,128]{3,2,1,0:T(8,128)S(1)}, u32[]{:S(2)}, u32[]{:S(2)}) collective-permute-start(f32[3,1,8,128]{3,2,1,0:T(8,128)S(1)} %get-tuple-element.32), channel_id=1, source_target_pairs={{16,0},{32,16},{48,32},{64,48},{80,64},{96,80},{112,96},{128,112},... | collective-permute-start | bytes 36872 | tf_op jit(solution)/shard_map/ppermute | solution.py:23
  166.3 5.9 collective-permute-start.1
  172.2 5.3 collective-permute-start.2
  173.5 4.8 collective-permute-start.3
  178.5 7.9 %collective-permute-start.5 = (f32[3,10,10,1]{3,2,1,0:T(8,128)S(1)}, f32[3,10,10,1]{3,2,1,0:T(8,128)S(1)}, u32[]{:S(2)}, u32[]{:S(2)}) collective-permute-start(f32[3,10,10,1]{3,2,1,0:T(8,128)S(1)} %get-tuple-element.20), channel_id=1, source_target_pairs={{0,1},{1,2},{2,3},{4,5},{5,6},{6,7},{8,9},{9,10},{10,11},{12,13},{... | collective-permute-start | bytes 3608 | tf_op jit(solution)/shard_map/ppermute | solution.py:20
  181.7 8.8 %collective-permute-start.4 = (f32[3,10,10,1]{3,2,1,0:T(8,128)S(1)}, f32[3,10,10,1]{3,2,1,0:T(8,128)S(1)}, u32[]{:S(2)}, u32[]{:S(2)}) collective-permute-start(f32[3,10,10,1]{3,2,1,0:T(8,128)S(1)} %get-tuple-element.19), channel_id=1, source_target_pairs={{1,0},{2,1},{3,2},{5,4},{6,5},{7,6},{9,8},{10,9},{11,10},{13,12},{... | collective-permute-start | bytes 3608 | tf_op jit(solution)/shard_map/ppermute | solution.py:23
  395.9 6.1 collective-permute-start.6
  398.5 4.3 collective-permute-start.7
  402.8 5.3 collective-permute-start.8
  404.1 4.8 collective-permute-start.9
  409.2 7.3 collective-permute-start.11
  411.7 8.6 %collective-permute-start.10 = (f32[3,10,10,1]{3,2,1,0:T(8,128)S(1)}, f32[3,10,10,1]{3,2,1,0:T(8,128)S(1)}, u32[]{:S(2)}, u32[]{:S(2)}) collective-permute-start(f32[3,10,10,1]{3,2,1,0:T(8,128)S(1)} %get-tuple-element.17), channel_id=1, source_target_pairs={{1,0},{2,1},{3,2},{5,4},{6,5},{7,6},{9,8},{10,9},{11,10},{13,12},{... | collective-permute-start | bytes 3608 | tf_op jit(solution)/shard_map/ppermute | solution.py:23
  625.2 5.6 collective-permute-start.12
  627.8 3.8 collective-permute-start.13
  631.6 5.3 collective-permute-start.14
  632.9 4.8 collective-permute-start.15
  637.9 7.1 collective-permute-start.17
  640.3 8.6 %collective-permute-start.16 = (f32[3,10,10,1]{3,2,1,0:T(8,128)S(1)}, f32[3,10,10,1]{3,2,1,0:T(8,128)S(1)}, u32[]{:S(2)}, u32[]{:S(2)}) collective-permute-start(f32[3,10,10,1]{3,2,1,0:T(8,128)S(1)} %get-tuple-element.15), channel_id=1, source_target_pairs={{1,0},{2,1},{3,2},{5,4},{6,5},{7,6},{9,8},{10,9},{11,10},{13,12},{... | collective-permute-start | bytes 3608 | tf_op jit(solution)/shard_map/ppermute | solution.py:23
